TPU v7x, 32 devices: a whole 2x2x4 slice. The times are simulated.
32 devices in a mesh: gx: 8 (over z, core), gy: 4 (over y, x).
Axes of the slice: x: 2, y: 2, z: 4, core: 2. Of those that a mesh axis runs over, the one named last changes fastest.
Arguments:
- residual: float32 [3, 128, 64, 128], P(None, 'gx', 'gy'), may hold values from -6 to 6
- stiffness: float32 [128, 64], P('gx', 'gy'), may hold values from 0.5 to 2
- local_inverse: bfloat16 [8, 4, 1024, 1024], P('gx', 'gy'), as said below
- coarse_basis: bfloat16 [8, 4, 8, 1024], P('gx', 'gy'), may hold values from -0.5 to 0.5
- coarse_rows: bfloat16 [8, 4, 8, 256], P('gx', 'gy'), as said below
- send_rows: int32 [8, 4, 4, 64], P('gx', 'gy'), may hold values from 0 to 767, as said below
- partition_map: int32 [32], replicated, may hold values from 0 to 31, as said below
Outputs:
- solution: float32 [3, 128, 64, 128], P(None, 'gx', 'gy')
- final: float32 [3, 128, 64, 128], P(None, 'gx', 'gy')
Inputs may be any that keep to these rules, and one draw needn't show every extreme that they name: `send_rows`: for each subdomain, the lists j = 0, 1 (lower and upper neighbour along gx) and j = 2, 3 (lower and upper neighbour along gy) each name 64 distinct owned rows, all of them in the two layers of cells nearest that neighbour. `partition_map`: A permutation of the device numbers. `coarse_rows`: with its columns put in device order through partition_map, the 256-square matrix S is symmetric. `local_inverse`: each subdomain's block is symmetric.
All inputs are finite; a program needn't handle non-finite values.
Results may differ from a plain program's by a relative error of at most 0.0057.
Values may be sent and summed in bfloat16 or wider, within the bound.
A program may use at most 64 MiB of HBM per device.

v0:
```python
import jax
import jax.numpy as jnp
from jax import lax
from jax.sharding import PartitionSpec as P


def with_halo(block, sides, width):
    for axis, dim in sides:
        count = lax.axis_size(axis)
        forward = [(i, i + 1) for i in range(count - 1)]
        backward = [(target, source) for source, target in forward]
        low = lax.ppermute(
            lax.slice_in_dim(block, block.shape[dim] - width, None, axis=dim), axis, forward
        )
        high = lax.ppermute(lax.slice_in_dim(block, 0, width, axis=dim), axis, backward)
        block = jnp.concatenate([low, block, high], axis=dim)
    return block


def trade_along_gx(pair):
    return with_halo(pair, (("gx", 0),), 1)


def trade_along_gy(pair):
    return with_halo(pair, (("gy", 0),), 1)


def operate(values, stiffness):
    padded = with_halo(values, (("gx", 1), ("gy", 2)), 1)
    beside = padded[:, 2:, 1:-1] + padded[:, :-2, 1:-1] + padded[:, 1:-1, 2:] + padded[:, 1:-1, :-2]
    return (4.0 + stiffness[None, :, :, None]) * values - beside


def coarse_solve(coarse_in, ordered):
    row_group = lax.all_gather(coarse_in, "gy", axis=0, tiled=True)
    return jnp.dot(
        ordered,
        lax.all_gather(row_group, "gx", axis=0, tiled=True),
        preferred_element_type=jnp.float32,
    )


def precondition(values, inverse, basis_rows, row_lists, ordered):
    own_rows = values.reshape(-1, values.shape[-1])
    own_count = own_rows.shape[0]
    margin = row_lists.shape[1]
    outgoing = jnp.take(own_rows, row_lists, axis=0)
    from_gx = trade_along_gx(outgoing[0:2])
    from_gy = trade_along_gy(outgoing[2:4])
    subdomain = jnp.concatenate([own_rows, from_gx[0], from_gx[3], from_gy[0], from_gy[3]], axis=0)
    subdomain = subdomain.astype(jnp.bfloat16)
    coarse_in = jnp.dot(basis_rows, subdomain, preferred_element_type=jnp.float32).astype(
        jnp.bfloat16
    )
    coarse_out = coarse_solve(coarse_in, ordered).astype(jnp.bfloat16)
    patch = jnp.dot(inverse, subdomain, preferred_element_type=jnp.float32)
    patch = patch + lax.dot_general(
        basis_rows, coarse_out, (((0,), (0,)), ((), ())), preferred_element_type=jnp.float32
    )
    back_gx = trade_along_gx(
        jnp.stack(
            [
                patch[own_count : own_count + margin],
                patch[own_count + margin : own_count + 2 * margin],
            ]
        )
    )
    back_gy = trade_along_gy(
        jnp.stack(
            [
                patch[own_count + 2 * margin : own_count + 3 * margin],
                patch[own_count + 3 * margin :],
            ]
        )
    )
    update = patch[:own_count]
    update = update.at[row_lists[0]].add(back_gx[0])
    update = update.at[row_lists[1]].add(back_gx[3])
    update = update.at[row_lists[2]].add(back_gy[0])
    update = update.at[row_lists[3]].add(back_gy[3])
    return update.reshape(values.shape)


def per_device(
    residual, stiffness, local_inverse, coarse_basis, coarse_rows, send_rows, partition_map
):
    inverse = local_inverse[0, 0]
    basis_rows = coarse_basis[0, 0]
    row_lists = send_rows[0, 0]
    device_count = partition_map.shape[0]
    coarse_width = basis_rows.shape[0]
    stored = coarse_rows[0, 0].reshape(coarse_width, device_count, coarse_width)
    ordered = jnp.take(stored, partition_map, axis=1).reshape(
        coarse_width, device_count * coarse_width
    )
    first_pass = precondition(residual, inverse, basis_rows, row_lists, ordered)
    middle = residual - operate(first_pass, stiffness)
    second_pass = precondition(middle, inverse, basis_rows, row_lists, ordered)
    solution = first_pass + second_pass
    return (solution, residual - operate(solution, stiffness))


def solution(mesh):
    placed = (
        P(None, "gx", "gy", None),
        P("gx", "gy"),
        P("gx", "gy", None, None),
        P("gx", "gy", None, None),
        P("gx", "gy", None, None),
        P("gx", "gy", None, None),
        P(),
    )
    return jax.shard_map(
        per_device,
        mesh=mesh,
        in_specs=placed,
        out_specs=(P(None, "gx", "gy", None), P(None, "gx", "gy", None)),
        check_vma=False,
    )
```

profile of v0, /device:TPU:21, one launch (start us, length us, event | category | flops | bytes accessed | tf_op | source)
XLA Modules:
  0.0 155.2 jit_solution(12951890438931751977)
XLA Ops:
  4.8 3.1 %collective-permute-start.3 = (bf16[1,64,128]{2,1,0:T(8,128)(2,1)S(1)}, bf16[1,64,128]{2,1,0:T(8,128)(2,1)S(1)}, u32[]{:S(2)}, u32[]{:S(2)}) collective-permute-start(bf16[1,64,128]{2,1,0:T(8,128)(2,1)S(1)} %get-tuple-element.23), channel_id=1, source_target_pairs={{1,0},{2,1},{3,2},{5,4},{6,5},{7,6},{9,8},{10,9},{11,10},{13,12},{... | collective-permute-start | bytes 49160 | tf_op jit(solution)/shard_map/ppermute | solution.py:15
  10.1 3.1 %collective-permute-start.1 = (bf16[1,64,128]{2,1,0:T(8,128)(2,1)S(1)}, bf16[1,64,128]{2,1,0:T(8,128)(2,1)S(1)}, u32[]{:S(2)}, u32[]{:S(2)}) collective-permute-start(bf16[1,64,128]{2,1,0:T(8,128)(2,1)S(1)} %get-tuple-element.25), channel_id=1, source_target_pairs={{4,0},{8,4},{12,8},{16,12},{20,16},{24,20},{28,24},{5,1},{9,5},{13... | collective-permute-start | bytes 49160 | tf_op jit(solution)/shard_map/ppermute | solution.py:15
  13.2 3.1 %collective-permute-start = (bf16[1,64,128]{2,1,0:T(8,128)(2,1)S(1)}, bf16[1,64,128]{2,1,0:T(8,128)(2,1)S(1)}, u32[]{:S(2)}, u32[]{:S(2)}) collective-permute-start(bf16[1,64,128]{2,1,0:T(8,128)(2,1)S(1)} %get-tuple-element.26), channel_id=1, source_target_pairs={{0,4},{4,8},{8,12},{12,16},{16,20},{20,24},{24,28},{1,5},{5,9},{9,... | collective-permute-start | bytes 49160 | tf_op jit(solution)/shard_map/ppermute | solution.py:12
  20.1 5.7 %all_gather.12 = bf16[32,128]{1,0:T(8,128)(2,1)S(1)} all-gather(bf16[8,128]{1,0:T(8,128)(2,1)S(1)} %fusion.16), channel_id=1, replica_groups=mesh['gx'=8,'gy'=4] {'gy'}, dimensions={0}, use_global_device_ids=true | all-gather | bytes 10240 | tf_op jit(solution)/shard_map/all_gather | solution.py:35
  25.8 13.1 %all_gather.13 = bf16[256,128]{1,0:T(8,128)(2,1)S(1)} all-gather(bf16[32,128]{1,0:T(8,128)(2,1)S(1)} %all_gather.12), channel_id=1, replica_groups=mesh['gx'=8,'gy'=4] {'gx'}, dimensions={0}, use_global_device_ids=true | all-gather | bytes 73728 | tf_op jit(solution)/shard_map/all_gather | solution.py:38
  40.9 3.1 %collective-permute-start.7 = (f32[1,64,128]{1,2,0:T(8,128)}, f32[1,64,128]{1,2,0:T(8,128)S(1)}, u32[]{:S(2)}, u32[]{:S(2)}) collective-permute-start(f32[1,64,128]{1,2,0:T(8,128)} %get-tuple-element.7), channel_id=1, source_target_pairs={{1,0},{2,1},{3,2},{5,4},{6,5},{7,6},{9,8},{10,9},{11,10},{13,12},{... | collective-permute-start | bytes 98312 | tf_op jit(solution)/shard_map/ppermute | solution.py:15
  46.2 2.6 %collective-permute-start.5 = (f32[1,64,128]{1,2,0:T(8,128)}, f32[1,64,128]{1,2,0:T(8,128)S(1)}, u32[]{:S(2)}, u32[]{:S(2)}) collective-permute-start(f32[1,64,128]{1,2,0:T(8,128)} %get-tuple-element.9), channel_id=1, source_target_pairs={{4,0},{8,4},{12,8},{16,12},{20,16},{24,20},{28,24},{5,1},{9,5},{13... | collective-permute-start | bytes 98312 | tf_op jit(solution)/shard_map/ppermute | solution.py:15
  48.8 4.9 %collective-permute-start.4 = (f32[1,64,128]{1,2,0:T(8,128)}, f32[1,64,128]{1,2,0:T(8,128)S(1)}, u32[]{:S(2)}, u32[]{:S(2)}) collective-permute-start(f32[1,64,128]{1,2,0:T(8,128)} %get-tuple-element.10), channel_id=1, source_target_pairs={{0,4},{4,8},{8,12},{12,16},{16,20},{20,24},{24,28},{1,5},{5,9},{9,... | collective-permute-start | bytes 98312 | tf_op jit(solution)/shard_map/ppermute | solution.py:12
  60.3 4.2 %collective-permute-start.9 = (f32[3,1,16,128]{3,2,1,0:T(8,128)S(1)}, f32[3,1,16,128]{3,2,1,0:T(8,128)S(1)}, u32[]{:S(2)}, u32[]{:S(2)}) collective-permute-start(f32[3,1,16,128]{3,2,1,0:T(8,128)S(1)} %get-tuple-element.17), channel_id=1, source_target_pairs={{0,4},{4,8},{8,12},{12,16},{16,20},{20,24},{24,28},{1,5},{5,9},{9,... | collective-permute-start | bytes 73736 | tf_op jit(solution)/shard_map/ppermute | solution.py:12
  66.4 3.2 %collective-permute-done.8 = f32[3,1,16,128]{3,2,1,0:T(8,128)S(1)} collective-permute-done((f32[3,1,16,128]{3,2,1,0:T(8,128)S(1)}, f32[3,1,16,128]{3,2,1,0:T(8,128)S(1)}, u32[]{:S(2)}, u32[]{:S(2)}) %collective-permute-start.8) | collective-permute-done | bytes 24608 | tf_op jit(solution)/shard_map/ppermute | solution.py:15
  69.6 4.0 %collective-permute-start.10 = (f32[3,18,1,128]{3,2,1,0:T(1,128)S(1)}, f32[3,18,1,128]{3,2,1,0:T(1,128)S(1)}, u32[]{:S(2)}, u32[]{:S(2)}) collective-permute-start(f32[3,18,1,128]{3,2,1,0:T(1,128)S(1)} %get-tuple-element.13), channel_id=1, source_target_pairs={{1,0},{2,1},{3,2},{5,4},{6,5},{7,6},{9,8},{10,9},{11,10},{13,12},{... | collective-permute-start | bytes 82952 | tf_op jit(solution)/shard_map/ppermute | solution.py:15
  75.6 3.5 %collective-permute-done.11 = f32[3,18,1,128]{3,2,1,0:T(1,128)S(1)} collective-permute-done((f32[3,18,1,128]{3,2,1,0:T(1,128)S(1)}, f32[3,18,1,128]{3,2,1,0:T(1,128)S(1)}, u32[]{:S(2)}, u32[]{:S(2)}) %collective-permute-start.11) | collective-permute-done | bytes 27680 | tf_op jit(solution)/shard_map/ppermute | solution.py:12
  80.3 3.4 %collective-permute-start.12 = (bf16[1,64,128]{2,1,0:T(8,128)(2,1)S(1)}, bf16[1,64,128]{2,1,0:T(8,128)(2,1)S(1)}, u32[]{:S(2)}, u32[]{:S(2)}) collective-permute-start(bf16[1,64,128]{2,1,0:T(8,128)(2,1)S(1)} %get-tuple-element.22), channel_id=1, source_target_pairs={{0,4},{4,8},{8,12},{12,16},{16,20},{20,24},{24,28},{1,5},{5,9},{9,... | collective-permute-start | bytes 49160 | tf_op jit(solution)/shard_map/ppermute | solution.py:12
  85.6 3.4 %collective-permute-start.14 = (bf16[1,64,128]{2,1,0:T(8,128)(2,1)S(1)}, bf16[1,64,128]{2,1,0:T(8,128)(2,1)S(1)}, u32[]{:S(2)}, u32[]{:S(2)}) collective-permute-start(bf16[1,64,128]{2,1,0:T(8,128)(2,1)S(1)} %get-tuple-element.20), channel_id=1, source_target_pairs={{0,1},{1,2},{2,3},{4,5},{5,6},{6,7},{8,9},{9,10},{10,11},{12,13},{... | collective-permute-start | bytes 49160 | tf_op jit(solution)/shard_map/ppermute | solution.py:12
  90.9 3.1 %collective-permute-done.13 = bf16[1,64,128]{2,1,0:T(8,128)(2,1)S(1)} collective-permute-done((bf16[1,64,128]{2,1,0:T(8,128)(2,1)S(1)}, bf16[1,64,128]{2,1,0:T(8,128)(2,1)S(1)}, u32[]{:S(2)}, u32[]{:S(2)}) %collective-permute-start.13) | collective-permute-done | bytes 16416 | tf_op jit(solution)/shard_map/ppermute | solution.py:15
  94.2 5.0 %all_gather.14 = bf16[32,128]{1,0:T(8,128)(2,1)S(1)} all-gather(bf16[8,128]{1,0:T(8,128)(2,1)S(1)} %fusion.17), channel_id=1, replica_groups=mesh['gx'=8,'gy'=4] {'gy'}, dimensions={0}, use_global_device_ids=true | all-gather | bytes 10240 | tf_op jit(solution)/shard_map/all_gather | solution.py:35
  99.3 12.5 %all_gather.15 = bf16[256,128]{1,0:T(8,128)(2,1)S(1)} all-gather(bf16[32,128]{1,0:T(8,128)(2,1)S(1)} %all_gather.14), channel_id=1, replica_groups=mesh['gx'=8,'gy'=4] {'gx'}, dimensions={0}, use_global_device_ids=true | all-gather | bytes 73728 | tf_op jit(solution)/shard_map/all_gather | solution.py:38
  114.7 3.1 %collective-permute-start.19 = (f32[1,64,128]{1,2,0:T(8,128)}, f32[1,64,128]{1,2,0:T(8,128)S(1)}, u32[]{:S(2)}, u32[]{:S(2)}) collective-permute-start(f32[1,64,128]{1,2,0:T(8,128)} %get-tuple-element.3), channel_id=1, source_target_pairs={{1,0},{2,1},{3,2},{5,4},{6,5},{7,6},{9,8},{10,9},{11,10},{13,12},{... | collective-permute-start | bytes 98312 | tf_op jit(solution)/shard_map/ppermute | solution.py:15
  120.0 2.6 %collective-permute-start.17 = (f32[1,64,128]{1,2,0:T(8,128)}, f32[1,64,128]{1,2,0:T(8,128)}, u32[]{:S(2)}, u32[]{:S(2)}) collective-permute-start(f32[1,64,128]{1,2,0:T(8,128)} %get-tuple-element.5), channel_id=1, source_target_pairs={{4,0},{8,4},{12,8},{16,12},{20,16},{24,20},{28,24},{5,1},{9,5},{13... | collective-permute-start | bytes 98312 | tf_op jit(solution)/shard_map/ppermute | solution.py:15
  122.7 4.8 %collective-permute-start.16 = (f32[1,64,128]{1,2,0:T(8,128)}, f32[1,64,128]{1,2,0:T(8,128)S(1)}, u32[]{:S(2)}, u32[]{:S(2)}) collective-permute-start(f32[1,64,128]{1,2,0:T(8,128)} %get-tuple-element.6), channel_id=1, source_target_pairs={{0,4},{4,8},{8,12},{12,16},{16,20},{20,24},{24,28},{1,5},{5,9},{9,... | collective-permute-start | bytes 98312 | tf_op jit(solution)/shard_map/ppermute | solution.py:12
  136.6 3.0 %collective-permute-start.21 = (f32[3,1,16,128]{3,2,1,0:T(8,128)S(1)}, f32[3,1,16,128]{3,2,1,0:T(8,128)S(1)}, u32[]{:S(2)}, u32[]{:S(2)}) collective-permute-start(f32[3,1,16,128]{3,2,1,0:T(8,128)S(1)} %get-tuple-element.15), channel_id=1, source_target_pairs={{0,4},{4,8},{8,12},{12,16},{16,20},{20,24},{24,28},{1,5},{5,9},{9,... | collective-permute-start | bytes 73736 | tf_op jit(solution)/shard_map/ppermute | solution.py:12
  141.5 3.2 %collective-permute-done.20 = f32[3,1,16,128]{3,2,1,0:T(8,128)S(1)} collective-permute-done((f32[3,1,16,128]{3,2,1,0:T(8,128)S(1)}, f32[3,1,16,128]{3,2,1,0:T(8,128)S(1)}, u32[]{:S(2)}, u32[]{:S(2)}) %collective-permute-start.20) | collective-permute-done | bytes 24608 | tf_op jit(solution)/shard_map/ppermute | solution.py:15
  144.8 4.0 %collective-permute-start.22 = (f32[3,18,1,128]{3,2,1,0:T(1,128)S(1)}, f32[3,18,1,128]{3,2,1,0:T(1,128)S(1)}, u32[]{:S(2)}, u32[]{:S(2)}) collective-permute-start(f32[3,18,1,128]{3,2,1,0:T(1,128)S(1)} %get-tuple-element.11), channel_id=1, source_target_pairs={{1,0},{2,1},{3,2},{5,4},{6,5},{7,6},{9,8},{10,9},{11,10},{13,12},{... | collective-permute-start | bytes 82952 | tf_op jit(solution)/shard_map/ppermute | solution.py:15
  150.7 3.6 %collective-permute-done.23 = f32[3,18,1,128]{3,2,1,0:T(1,128)S(1)} collective-permute-done((f32[3,18,1,128]{3,2,1,0:T(1,128)S(1)}, f32[3,18,1,128]{3,2,1,0:T(1,128)S(1)}, u32[]{:S(2)}, u32[]{:S(2)}) %collective-permute-start.23) | collective-permute-done | bytes 27680 | tf_op jit(solution)/shard_map/ppermute | solution.py:12
  (134 shorter events, 48.6 us)
Async XLA Ops:
  4.8 15.1 %collective-permute-start.3 = (bf16[1,64,128]{2,1,0:T(8,128)(2,1)S(1)}, bf16[1,64,128]{2,1,0:T(8,128)(2,1)S(1)}, u32[]{:S(2)}, u32[]{:S(2)}) collective-permute-start(bf16[1,64,128]{2,1,0:T(8,128)(2,1)S(1)} %get-tuple-element.23), channel_id=1, source_target_pairs={{1,0},{2,1},{3,2},{5,4},{6,5},{7,6},{9,8},{10,9},{11,10},{13,12},{... | collective-permute-start | bytes 49160 | tf_op jit(solution)/shard_map/ppermute | solution.py:15
  7.9 12.0 %collective-permute-start.2 = (bf16[1,64,128]{2,1,0:T(8,128)(2,1)S(1)}, bf16[1,64,128]{2,1,0:T(8,128)(2,1)S(1)}, u32[]{:S(2)}, u32[]{:S(2)}) collective-permute-start(bf16[1,64,128]{2,1,0:T(8,128)(2,1)S(1)} %get-tuple-element.24), channel_id=1, source_target_pairs={{0,1},{1,2},{2,3},{4,5},{5,6},{6,7},{8,9},{9,10},{10,11},{12,13},{... | collective-permute-start | bytes 49160 | tf_op jit(solution)/shard_map/ppermute | solution.py:12
  10.1 9.7 %collective-permute-start.1 = (bf16[1,64,128]{2,1,0:T(8,128)(2,1)S(1)}, bf16[1,64,128]{2,1,0:T(8,128)(2,1)S(1)}, u32[]{:S(2)}, u32[]{:S(2)}) collective-permute-start(bf16[1,64,128]{2,1,0:T(8,128)(2,1)S(1)} %get-tuple-element.25), channel_id=1, source_target_pairs={{4,0},{8,4},{12,8},{16,12},{20,16},{24,20},{28,24},{5,1},{9,5},{13... | collective-permute-start | bytes 49160 | tf_op jit(solution)/shard_map/ppermute | solution.py:15
  13.2 6.6 %collective-permute-start = (bf16[1,64,128]{2,1,0:T(8,128)(2,1)S(1)}, bf16[1,64,128]{2,1,0:T(8,128)(2,1)S(1)}, u32[]{:S(2)}, u32[]{:S(2)}) collective-permute-start(bf16[1,64,128]{2,1,0:T(8,128)(2,1)S(1)} %get-tuple-element.26), channel_id=1, source_target_pairs={{0,4},{4,8},{8,12},{12,16},{16,20},{20,24},{24,28},{1,5},{5,9},{9,... | collective-permute-start | bytes 49160 | tf_op jit(solution)/shard_map/ppermute | solution.py:12
  40.9 13.6 %collective-permute-start.7 = (f32[1,64,128]{1,2,0:T(8,128)}, f32[1,64,128]{1,2,0:T(8,128)S(1)}, u32[]{:S(2)}, u32[]{:S(2)}) collective-permute-start(f32[1,64,128]{1,2,0:T(8,128)} %get-tuple-element.7), channel_id=1, source_target_pairs={{1,0},{2,1},{3,2},{5,4},{6,5},{7,6},{9,8},{10,9},{11,10},{13,12},{... | collective-permute-start | bytes 98312 | tf_op jit(solution)/shard_map/ppermute | solution.py:15
  43.9 10.6 %collective-permute-start.6 = (f32[1,64,128]{1,2,0:T(8,128)}, f32[1,64,128]{1,2,0:T(8,128)S(1)}, u32[]{:S(2)}, u32[]{:S(2)}) collective-permute-start(f32[1,64,128]{1,2,0:T(8,128)} %get-tuple-element.8), channel_id=1, source_target_pairs={{0,1},{1,2},{2,3},{4,5},{5,6},{6,7},{8,9},{9,10},{10,11},{12,13},{... | collective-permute-start | bytes 98312 | tf_op jit(solution)/shard_map/ppermute | solution.py:12
  46.2 8.5 %collective-permute-start.5 = (f32[1,64,128]{1,2,0:T(8,128)}, f32[1,64,128]{1,2,0:T(8,128)S(1)}, u32[]{:S(2)}, u32[]{:S(2)}) collective-permute-start(f32[1,64,128]{1,2,0:T(8,128)} %get-tuple-element.9), channel_id=1, source_target_pairs={{4,0},{8,4},{12,8},{16,12},{20,16},{24,20},{28,24},{5,1},{9,5},{13... | collective-permute-start | bytes 98312 | tf_op jit(solution)/shard_map/ppermute | solution.py:15
  48.8 6.5 %collective-permute-start.4 = (f32[1,64,128]{1,2,0:T(8,128)}, f32[1,64,128]{1,2,0:T(8,128)S(1)}, u32[]{:S(2)}, u32[]{:S(2)}) collective-permute-start(f32[1,64,128]{1,2,0:T(8,128)} %get-tuple-element.10), channel_id=1, source_target_pairs={{0,4},{4,8},{8,12},{12,16},{16,20},{20,24},{24,28},{1,5},{5,9},{9,... | collective-permute-start | bytes 98312 | tf_op jit(solution)/shard_map/ppermute | solution.py:12
  60.3 6.1 %collective-permute-start.9 = (f32[3,1,16,128]{3,2,1,0:T(8,128)S(1)}, f32[3,1,16,128]{3,2,1,0:T(8,128)S(1)}, u32[]{:S(2)}, u32[]{:S(2)}) collective-permute-start(f32[3,1,16,128]{3,2,1,0:T(8,128)S(1)} %get-tuple-element.17), channel_id=1, source_target_pairs={{0,4},{4,8},{8,12},{12,16},{16,20},{20,24},{24,28},{1,5},{5,9},{9,... | collective-permute-start | bytes 73736 | tf_op jit(solution)/shard_map/ppermute | solution.py:12
  64.4 5.1 %collective-permute-start.8 = (f32[3,1,16,128]{3,2,1,0:T(8,128)S(1)}, f32[3,1,16,128]{3,2,1,0:T(8,128)S(1)}, u32[]{:S(2)}, u32[]{:S(2)}) collective-permute-start(f32[3,1,16,128]{3,2,1,0:T(8,128)S(1)} %get-tuple-element.18), channel_id=1, source_target_pairs={{4,0},{8,4},{12,8},{16,12},{20,16},{24,20},{28,24},{5,1},{9,5},{13... | collective-permute-start | bytes 73736 | tf_op jit(solution)/shard_map/ppermute | solution.py:15
  69.6 5.9 %collective-permute-start.10 = (f32[3,18,1,128]{3,2,1,0:T(1,128)S(1)}, f32[3,18,1,128]{3,2,1,0:T(1,128)S(1)}, u32[]{:S(2)}, u32[]{:S(2)}) collective-permute-start(f32[3,18,1,128]{3,2,1,0:T(1,128)S(1)} %get-tuple-element.13), channel_id=1, source_target_pairs={{1,0},{2,1},{3,2},{5,4},{6,5},{7,6},{9,8},{10,9},{11,10},{13,12},{... | collective-permute-start | bytes 82952 | tf_op jit(solution)/shard_map/ppermute | solution.py:15
  73.6 5.5 %collective-permute-start.11 = (f32[3,18,1,128]{3,2,1,0:T(1,128)S(1)}, f32[3,18,1,128]{3,2,1,0:T(1,128)S(1)}, u32[]{:S(2)}, u32[]{:S(2)}) collective-permute-start(f32[3,18,1,128]{3,2,1,0:T(1,128)S(1)} %get-tuple-element.14), channel_id=1, source_target_pairs={{0,1},{1,2},{2,3},{4,5},{5,6},{6,7},{8,9},{9,10},{10,11},{12,13},{... | collective-permute-start | bytes 82952 | tf_op jit(solution)/shard_map/ppermute | solution.py:12
  80.3 10.6 %collective-permute-start.12 = (bf16[1,64,128]{2,1,0:T(8,128)(2,1)S(1)}, bf16[1,64,128]{2,1,0:T(8,128)(2,1)S(1)}, u32[]{:S(2)}, u32[]{:S(2)}) collective-permute-start(bf16[1,64,128]{2,1,0:T(8,128)(2,1)S(1)} %get-tuple-element.22), channel_id=1, source_target_pairs={{0,4},{4,8},{8,12},{12,16},{16,20},{20,24},{24,28},{1,5},{5,9},{9,... | collective-permute-start | bytes 49160 | tf_op jit(solution)/shard_map/ppermute | solution.py:12
  83.7 10.4 %collective-permute-start.15 = (bf16[1,64,128]{2,1,0:T(8,128)(2,1)S(1)}, bf16[1,64,128]{2,1,0:T(8,128)(2,1)S(1)}, u32[]{:S(2)}, u32[]{:S(2)}) collective-permute-start(bf16[1,64,128]{2,1,0:T(8,128)(2,1)S(1)} %get-tuple-element.19), channel_id=1, source_target_pairs={{1,0},{2,1},{3,2},{5,4},{6,5},{7,6},{9,8},{10,9},{11,10},{13,12},{... | collective-permute-start | bytes 49160 | tf_op jit(solution)/shard_map/ppermute | solution.py:15
  85.6 8.4 %collective-permute-start.14 = (bf16[1,64,128]{2,1,0:T(8,128)(2,1)S(1)}, bf16[1,64,128]{2,1,0:T(8,128)(2,1)S(1)}, u32[]{:S(2)}, u32[]{:S(2)}) collective-permute-start(bf16[1,64,128]{2,1,0:T(8,128)(2,1)S(1)} %get-tuple-element.20), channel_id=1, source_target_pairs={{0,1},{1,2},{2,3},{4,5},{5,6},{6,7},{8,9},{9,10},{10,11},{12,13},{... | collective-permute-start | bytes 49160 | tf_op jit(solution)/shard_map/ppermute | solution.py:12
  89.0 5.1 %collective-permute-start.13 = (bf16[1,64,128]{2,1,0:T(8,128)(2,1)S(1)}, bf16[1,64,128]{2,1,0:T(8,128)(2,1)S(1)}, u32[]{:S(2)}, u32[]{:S(2)}) collective-permute-start(bf16[1,64,128]{2,1,0:T(8,128)(2,1)S(1)} %get-tuple-element.21), channel_id=1, source_target_pairs={{4,0},{8,4},{12,8},{16,12},{20,16},{24,20},{28,24},{5,1},{9,5},{13... | collective-permute-start | bytes 49160 | tf_op jit(solution)/shard_map/ppermute | solution.py:15
  114.7 14.7 %collective-permute-start.19 = (f32[1,64,128]{1,2,0:T(8,128)}, f32[1,64,128]{1,2,0:T(8,128)S(1)}, u32[]{:S(2)}, u32[]{:S(2)}) collective-permute-start(f32[1,64,128]{1,2,0:T(8,128)} %get-tuple-element.3), channel_id=1, source_target_pairs={{1,0},{2,1},{3,2},{5,4},{6,5},{7,6},{9,8},{10,9},{11,10},{13,12},{... | collective-permute-start | bytes 98312 | tf_op jit(solution)/shard_map/ppermute | solution.py:15
  117.8 13.2 %collective-permute-start.18 = (f32[1,64,128]{1,2,0:T(8,128)}, f32[1,64,128]{1,2,0:T(8,128)S(1)}, u32[]{:S(2)}, u32[]{:S(2)}) collective-permute-start(f32[1,64,128]{1,2,0:T(8,128)} %get-tuple-element.4), channel_id=1, source_target_pairs={{0,1},{1,2},{2,3},{4,5},{5,6},{6,7},{8,9},{9,10},{10,11},{12,13},{... | collective-permute-start | bytes 98312 | tf_op jit(solution)/shard_map/ppermute | solution.py:12
  120.0 11.1 %collective-permute-start.17 = (f32[1,64,128]{1,2,0:T(8,128)}, f32[1,64,128]{1,2,0:T(8,128)}, u32[]{:S(2)}, u32[]{:S(2)}) collective-permute-start(f32[1,64,128]{1,2,0:T(8,128)} %get-tuple-element.5), channel_id=1, source_target_pairs={{4,0},{8,4},{12,8},{16,12},{20,16},{24,20},{28,24},{5,1},{9,5},{13... | collective-permute-start | bytes 98312 | tf_op jit(solution)/shard_map/ppermute | solution.py:15
  122.7 9.4 %collective-permute-start.16 = (f32[1,64,128]{1,2,0:T(8,128)}, f32[1,64,128]{1,2,0:T(8,128)S(1)}, u32[]{:S(2)}, u32[]{:S(2)}) collective-permute-start(f32[1,64,128]{1,2,0:T(8,128)} %get-tuple-element.6), channel_id=1, source_target_pairs={{0,4},{4,8},{8,12},{12,16},{16,20},{20,24},{24,28},{1,5},{5,9},{9,... | collective-permute-start | bytes 98312 | tf_op jit(solution)/shard_map/ppermute | solution.py:12
  136.6 4.9 %collective-permute-start.21 = (f32[3,1,16,128]{3,2,1,0:T(8,128)S(1)}, f32[3,1,16,128]{3,2,1,0:T(8,128)S(1)}, u32[]{:S(2)}, u32[]{:S(2)}) collective-permute-start(f32[3,1,16,128]{3,2,1,0:T(8,128)S(1)} %get-tuple-element.15), channel_id=1, source_target_pairs={{0,4},{4,8},{8,12},{12,16},{16,20},{20,24},{24,28},{1,5},{5,9},{9,... | collective-permute-start | bytes 73736 | tf_op jit(solution)/shard_map/ppermute | solution.py:12
  139.6 5.1 %collective-permute-start.20 = (f32[3,1,16,128]{3,2,1,0:T(8,128)S(1)}, f32[3,1,16,128]{3,2,1,0:T(8,128)S(1)}, u32[]{:S(2)}, u32[]{:S(2)}) collective-permute-start(f32[3,1,16,128]{3,2,1,0:T(8,128)S(1)} %get-tuple-element.16), channel_id=1, source_target_pairs={{4,0},{8,4},{12,8},{16,12},{20,16},{24,20},{28,24},{5,1},{9,5},{13... | collective-permute-start | bytes 73736 | tf_op jit(solution)/shard_map/ppermute | solution.py:15
  144.8 5.9 %collective-permute-start.22 = (f32[3,18,1,128]{3,2,1,0:T(1,128)S(1)}, f32[3,18,1,128]{3,2,1,0:T(1,128)S(1)}, u32[]{:S(2)}, u32[]{:S(2)}) collective-permute-start(f32[3,18,1,128]{3,2,1,0:T(1,128)S(1)} %get-tuple-element.11), channel_id=1, source_target_pairs={{1,0},{2,1},{3,2},{5,4},{6,5},{7,6},{9,8},{10,9},{11,10},{13,12},{... | collective-permute-start | bytes 82952 | tf_op jit(solution)/shard_map/ppermute | solution.py:15
  148.8 5.5 %collective-permute-start.23 = (f32[3,18,1,128]{3,2,1,0:T(1,128)S(1)}, f32[3,18,1,128]{3,2,1,0:T(1,128)S(1)}, u32[]{:S(2)}, u32[]{:S(2)}) collective-permute-start(f32[3,18,1,128]{3,2,1,0:T(1,128)S(1)} %get-tuple-element.12), channel_id=1, source_target_pairs={{0,1},{1,2},{2,3},{4,5},{5,6},{6,7},{8,9},{9,10},{10,11},{12,13},{... | collective-permute-start | bytes 82952 | tf_op jit(solution)/shard_map/ppermute | solution.py:12
  (20 other events, 454.2 us)
where the time goes:
time: 156 us; the launch traced here: 155 us
  starting transfers between devices  70.4 us (45%)
  blocking collectives  36.3 us (23%)
  waiting for transfers between devices  17.3 us (11%)
  other arithmetic  15 us (10%)
  local copies, waits for them, and re-layouts  11.1 us (7%)
  matrix products  3.7 us (2%)
    ppermute x12, starting transfers between devices, with_halo(): lax.ppermute(lax.slice_in_dim(block, block.shape[dim] - width, None, axis...  37.1 us
    ppermute x12, starting transfers between devices, with_halo(): lax.ppermute(lax.slice_in_dim(block, 0, width, axis=dim), axis, backward)  33.3 us
    all_gather x2, blocking collectives, coarse_solve(): lax.all_gather(row_group, 'gx', axis=0, tiled=True)  25.5 us
    all_gather x2, blocking collectives, coarse_solve(): row_group = lax.all_gather(coarse_in, 'gy', axis=0, tiled=True)  10.7 us
    ppermute x12, waiting for transfers between devices, with_halo(): lax.ppermute(lax.slice_in_dim(block, 0, width, axis=dim), axis, backward)  9.56 us
    ppermute x12, waiting for transfers between devices, with_halo(): lax.ppermute(lax.slice_in_dim(block, block.shape[dim] - width, None, axis...  7.72 us
  transfers between devices with their start and end apart: 24, of which 6 were waited for; matrix products, arithmetic and copies ran while one was open for 5% of the time, Pallas kernels for 0%

commit v1 on v0

v1 whole, which is shorter than its diff:
```python
import functools

import jax
import jax.numpy as jnp
from jax import lax
from jax.experimental import pallas as pl
from jax.experimental.pallas import tpu as pltpu
from jax.sharding import PartitionSpec as P

MESH = pl.DeviceIdType.MESH
F32 = jnp.float32
BF16 = jnp.bfloat16
HIGH = lax.Precision.HIGHEST


def dot(x, y, **kw):
    return jnp.dot(x, y, preferred_element_type=F32, **kw)


def tdot(x, y):
    return lax.dot_general(x, y, (((0,), (0,)), ((), ())), preferred_element_type=F32)


def fiota(shape, axis):
    return lax.broadcasted_iota(jnp.int32, shape, axis).astype(F32)


def fdiv(x, n):
    return jnp.floor((x + 0.5) * (1.0 / n))


def kernel(
    gx, gy, dims,
    res_hbm, stiff_ref, inv_hbm, basis_ref, crows_ref, lists_ref, pmap_ref,
    sol_ref, fin_ref,
    res_v, inv_v, sub, sel, selt, outs, backs, backr, hs, hr, allbuf,
    sext, bsend, brecv, bext, diag, m_lo, m_hi, xs, mid,
    lsem, nsem_s, nsem_r, csem_s, csem_r, g1s, g1r, g2s, g2r,
):
    comps, cx, cy, nv = dims
    own = comps * cx * cy
    layer = cx * cy
    ov = lists_ref.shape[1]
    kw, kd = crows_ref.shape
    a = lax.axis_index("gx")
    b = lax.axis_index("gy")

    load_res = pltpu.make_async_copy(res_hbm, res_v, lsem.at[0])
    load_inv = pltpu.make_async_copy(inv_hbm, inv_v, lsem.at[1])
    load_res.start()
    load_inv.start()

    barrier = pltpu.get_barrier_semaphore()
    for o in range(1, gx):
        pl.semaphore_signal(barrier, inc=1, device_id=(lax.rem(a + o, gx), b), device_id_type=MESH)
    for o in range(1, gy):
        pl.semaphore_signal(barrier, inc=1, device_id=(a, lax.rem(b + o, gy)), device_id_type=MESH)

    up = [(a + 1, b), (a - 1, b), (a, b + 1), (a, b - 1)]
    has_up = [a < gx - 1, a > 0, b < gy - 1, b > 0]
    down = [up[p ^ 1] for p in range(4)]
    has_down = [has_up[p ^ 1] for p in range(4)]
    finish = []

    def send(copies, conds, wait):
        for p in range(4):
            @pl.when(conds[p])
            def _(p=p):
                for c in copies(p):
                    getattr(c, wait)()

    def trade(copies, forward):
        to, fro = (has_up, has_down) if forward else (has_down, has_up)
        send(copies, to, "start")
        finish.append(lambda: send(copies, to, "wait_send"))
        return lambda: send(copies, fro, "wait_recv")

    def remote(src, dst, s, r, dev):
        return pltpu.make_async_remote_copy(
            src_ref=src, dst_ref=dst, send_sem=s, recv_sem=r, device_id=dev, device_id_type=MESH
        )

    rows = fiota((own, ov), 0)
    lists = lists_ref[...].astype(F32)
    for h in range(2):
        two = [jnp.where(rows == lists[p ^ 1 : (p ^ 1) + 1], 1.0, 0.0) for p in (2 * h, 2 * h + 1)]
        both = jnp.concatenate(two, axis=1)
        sel[:, 2 * ov * h : 2 * ov * (h + 1)] = both.astype(BF16)
        selt[2 * ov * h : 2 * ov * (h + 1), :] = both.T.astype(BF16)

    for p in range(4):
        at = own + p * ov

        @pl.when(jnp.logical_not(has_down[p]))
        def _(p=p, at=at):
            for t in range(2):
                sub[t, at : at + ov, :] = jnp.zeros((ov, nv), BF16)
                hr[t, p] = jnp.zeros(hr.shape[2:], F32)

        @pl.when(jnp.logical_not(has_up[p]))
        def _(p=p):
            for t in range(2):
                backr[t, p * ov : (p + 1) * ov, :] = jnp.zeros((ov, nv), BF16)
            sext[(p + 1) * kw : (p + 2) * kw, :] = jnp.zeros((kw, kd), F32)
            brecv[p * kw : (p + 1) * kw, :] = jnp.zeros((kw, 4 * ov), F32)

    load_res.wait()

    def gather(t, src):
        value = src[...].astype(BF16)
        sub[t, :own, :] = value
        outs[t] = dot(selt[...], value).astype(BF16)

    gather(0, res_v)
    pl.semaphore_wait(barrier, gx + gy - 2)

    def start_margins(t):
        return trade(
            lambda p: [remote(outs.at[t, pl.ds(p * ov, ov)], sub.at[t, pl.ds(own + p * ov, ov)],
                              nsem_s.at[t, 0, p], nsem_r.at[t, 0, p], up[p])],
            True,
        )

    wait_margins = start_margins(0)

    wide = min(kd, 256)
    n = gx * gy
    pmf = jnp.broadcast_to(pmap_ref[...].astype(F32), (8, n))

    def order(c, _):
        q = fiota((1, wide), 1) + (c * wide).astype(F32)
        slot = fdiv(q, kw)
        slab = fdiv(slot, gx)
        dev = (slot - slab * gx) * gy + slab
        pick = jnp.where(fiota((n, wide), 0) == dev, 1.0, 0.0)
        place = dot(pmf, pick, precision=HIGH)[0:1] * kw + (q - slot * kw)
        perm = jnp.where(fiota((kd, wide), 0) == place, 1.0, 0.0).astype(BF16)
        sext[0:kw, pl.ds(pl.multiple_of(c * wide, wide), wide)] = dot(crows_ref[...], perm)
        return 0

    lax.fori_loop(jnp.int32(0), jnp.int32(kd // wide), order, 0)
    bsend[...] = basis_ref[:, own:].astype(F32)
    wait_coarse = trade(
        lambda p: [
            remote(sext.at[pl.ds(0, kw)], sext.at[pl.ds((p + 1) * kw, kw)], csem_s.at[0, p], csem_r.at[0, p], down[p]),
            remote(bsend, brecv.at[pl.ds(p * kw, kw)], csem_s.at[1, p], csem_r.at[1, p], down[p]),
        ],
        False,
    )

    r1 = fiota((layer, cy), 0)
    first = fdiv(r1, cy)
    mine = jnp.where(fiota((layer, cx), 1) == fdiv(fiota((layer, cx), 0), cy), 1.0, 0.0)
    spread = dot(mine, stiff_ref[...], precision=HIGH)
    spread = jnp.where(fiota((layer, cy), 1) == r1 - first * cy, spread, 0.0)
    diag[...] = jnp.broadcast_to(4.0 + jnp.sum(spread, axis=1, keepdims=True), (layer, nv))
    rr = fiota((layer, nv), 0)
    second = rr - fdiv(rr, cy) * cy
    m_lo[...] = jnp.where(second == 0.0, 0.0, 1.0)
    m_hi[...] = jnp.where(second == cy - 1.0, 0.0, 1.0)

    def correct(t, src, dst, wait_margins):
        if t == 0:
            load_inv.wait()
        part = dot(inv_v[:, :own], sub[t, :own, :])
        cpart = dot(basis_ref[:, :own], sub[t, :own, :])
        wait_margins()
        edge = sub[t, own:, :]
        cin = cpart + dot(basis_ref[:, own:], edge)
        allbuf[t, b, a] = cin.astype(BF16)

        def stage1(o, dev, slot):
            ref = allbuf.at[t, b, slot]
            return remote(ref, ref, g1s.at[t, o], g1r.at[t, o], (dev, b))

        def stage2(o, dev, slot):
            ref = allbuf.at[t, slot]
            return remote(ref, ref, g2s.at[t, o], g2r.at[t, o], (a, dev))

        for o in range(1, gx):
            stage1(o, lax.rem(a + o, gx), a).start()
        patch = part + dot(inv_v[:, own:], edge)
        backs[t] = patch[own:].astype(BF16)
        wait_back = trade(
            lambda p: [remote(backs.at[t, pl.ds(p * ov, ov)], backr.at[t, pl.ds(p * ov, ov)],
                              nsem_s.at[t, 1, p], nsem_r.at[t, 1, p], down[p])],
            False,
        )
        xs[...] = patch[:own]
        for o in range(1, gx):
            stage1(o, lax.rem(a + o, gx), lax.rem(a + (gx - o), gx)).wait_recv()
        for o in range(1, gy):
            stage2(o, lax.rem(b + o, gy), b).start()
        if t == 0:
            wait_coarse()
            rb = fdiv(fiota((4 * kw, 4 * ov), 0), kw)
            cb = fdiv(fiota((4 * kw, 4 * ov), 1), ov)
            margins = jnp.where(rb == cb, brecv[...], 0.0).astype(BF16)
            below = dot(margins, selt[...])
            ext = jnp.concatenate([basis_ref[:, :own].astype(F32), below], axis=0)
            bext[...] = ext.T.astype(BF16)
        wait_back()
        xs[...] += dot(sel[...], backr[t])
        for o in range(1, gy):
            stage2(o, lax.rem(b + o, gy), lax.rem(b + (gy - o), gy)).wait_recv()
        gathered = allbuf[t].astype(F32).reshape(kd, nv).astype(BF16)
        cout = dot(sext[...].astype(BF16), gathered).astype(BF16)
        xs[...] += dot(bext[...], cout)

        def done():
            for o in range(1, gx):
                stage1(o, lax.rem(a + o, gx), a).wait_send()
            for o in range(1, gy):
                stage2(o, lax.rem(b + o, gy), b).wait_send()

        finish.append(done)

        for c in range(comps):
            base = c * layer
            hs[t, 0, c * cy : (c + 1) * cy, :] = xs[base + layer - cy : base + layer, :]
            hs[t, 1, c * cy : (c + 1) * cy, :] = xs[base : base + cy, :]
        hs[t, 2, : comps * cx, :] = xs[pl.ds(cy - 1, comps * cx, stride=cy), :]
        hs[t, 3, : comps * cx, :] = xs[pl.ds(0, comps * cx, stride=cy), :]
        wait_halo = trade(
            lambda p: [remote(hs.at[t, p], hr.at[t, p], nsem_s.at[t, 2, p], nsem_r.at[t, 2, p], up[p])],
            True,
        )
        zero = jnp.zeros((cy, nv), F32)
        for c in range(comps):
            at = pl.ds(c * layer, layer)
            x = xs[at, :]
            beside = jnp.concatenate([zero, x[:-cy]], axis=0) + jnp.concatenate([x[cy:], zero], axis=0)
            beside += pltpu.roll(x, 1, 0) * m_lo[...] + pltpu.roll(x, layer - 1, 0) * m_hi[...]
            dst[at, :] = src[at, :] - (diag[...] * x - beside)
        return wait_halo

    def finish_halo(t, dst, wait_halo):
        wait_halo()
        for c in range(comps):
            base = c * layer
            dst[base : base + cy, :] += hr[t, 0, c * cy : (c + 1) * cy, :]
            dst[base + layer - cy : base + layer, :] += hr[t, 1, c * cy : (c + 1) * cy, :]
        low = pl.ds(0, comps * cx, stride=cy)
        high = pl.ds(cy - 1, comps * cx, stride=cy)
        dst[low, :] = dst[low, :] + hr[t, 2, : comps * cx, :]
        dst[high, :] = dst[high, :] + hr[t, 3, : comps * cx, :]

    wait_halo = correct(0, res_v, mid, wait_margins)
    sol_ref[...] = xs[...]
    finish_halo(0, mid, wait_halo)
    gather(1, mid)
    wait_halo = correct(1, mid, fin_ref, start_margins(1))
    sol_ref[...] += xs[...]
    finish_halo(1, fin_ref, wait_halo)
    for end in finish:
        end()


def solution(mesh):
    gx, gy = mesh.shape["gx"], mesh.shape["gy"]

    def per_device(residual, stiffness, local_inverse, coarse_basis, coarse_rows, send_rows, partition_map):
        comps, cx, cy, nv = residual.shape
        own, layer = comps * cx * cy, cx * cy
        m = local_inverse.shape[-1]
        ov = send_rows.shape[-1]
        kw, kd = coarse_rows.shape[-2:]
        halo = comps * max(cx, cy)
        vm = pl.BlockSpec(memory_space=pltpu.VMEM)
        anywhere = pl.BlockSpec(memory_space=pl.ANY)
        dma = pltpu.SemaphoreType.DMA
        out = pl.pallas_call(
            functools.partial(kernel, gx, gy, (comps, cx, cy, nv)),
            out_shape=[jax.ShapeDtypeStruct((own, nv), F32)] * 2,
            in_specs=[anywhere, vm, anywhere, vm, vm, vm, vm],
            out_specs=[vm, vm],
            scratch_shapes=[
                pltpu.VMEM((own, nv), F32),
                pltpu.VMEM((m, m), BF16),
                pltpu.VMEM((2, m, nv), BF16),
                pltpu.VMEM((own, 4 * ov), BF16),
                pltpu.VMEM((4 * ov, own), BF16),
                pltpu.VMEM((2, 4 * ov, nv), BF16),
                pltpu.VMEM((2, 4 * ov, nv), BF16),
                pltpu.VMEM((2, 4 * ov, nv), BF16),
                pltpu.VMEM((2, 4, halo, nv), F32),
                pltpu.VMEM((2, 4, halo, nv), F32),
                pltpu.VMEM((2, gy, gx, kw, nv), BF16),
                pltpu.VMEM((5 * kw, kd), F32),
                pltpu.VMEM((kw, m - own), F32),
                pltpu.VMEM((4 * kw, m - own), F32),
                pltpu.VMEM((own, 5 * kw), BF16),
                pltpu.VMEM((layer, nv), F32),
                pltpu.VMEM((layer, nv), F32),
                pltpu.VMEM((layer, nv), F32),
                pltpu.VMEM((own, nv), F32),
                pltpu.VMEM((own, nv), F32),
                dma((2,)),
                dma((2, 3, 4)),
                dma((2, 3, 4)),
                dma((2, 4)),
                dma((2, 4)),
                dma((2, gx)),
                dma((2, gx)),
                dma((2, gy)),
                dma((2, gy)),
            ],
            compiler_params=pltpu.CompilerParams(collective_id=0, has_side_effects=True),
        )(
            residual.reshape(own, nv),
            stiffness,
            local_inverse[0, 0],
            coarse_basis[0, 0],
            coarse_rows[0, 0],
            send_rows[0, 0],
            partition_map.reshape(1, -1),
        )
        return tuple(o.reshape(residual.shape) for o in out)

    placed = (
        P(None, "gx", "gy", None),
        P("gx", "gy"),
        P("gx", "gy", None, None),
        P("gx", "gy", None, None),
        P("gx", "gy", None, None),
        P("gx", "gy", None, None),
        P(),
    )
    return jax.shard_map(
        per_device,
        mesh=mesh,
        in_specs=placed,
        out_specs=(P(None, "gx", "gy", None), P(None, "gx", "gy", None)),
        check_vma=False,
    )
```

time: 156 us -> 41.2 us (0.26)
  the two profiles are of different devices: /device:TPU:21 before, /device:TPU:0 now
where the time goes in v1:
time: 41.2 us; the launch traced here: 40.9 us
  Pallas kernels  36.7 us (89%)
  local copies, waits for them, and re-layouts  3.53 us (9%)
  between operations  0.64 us (2%)
    pallas_call x1, Pallas kernels, per_device(): pl.pallas_call(functools.partial(kernel, gx, gy, (comps, cx, cy, nv)), ou...  36.7 us
    unnamed x2, local copies, waits for them, and re-layouts  3.53 us

profile of v1, /device:TPU:0, one launch (start us, length us, event | category | flops | bytes accessed | tf_op | source)
XLA Modules:
  0.0 40.9 jit_solution(1451185767088636449)
XLA Ops:
  0.6 36.7 %shard_map.86 = (f32[768,128]{1,0:T(8,128)}, f32[768,128]{1,0:T(8,128)}) custom-call(f32[768,128]{1,0:T(8,128)} %bitcast.9, f32[16,16]{1,0:T(8,128)} %stiff_ref.1, bf16[1024,1024]{1,0:T(8,128)(2,1)} %bitcast.8, bf16[8,1024]{1,0:T(8,128)(2,1)} %bitcast.12, bf16[8,256]{1,0:T(8,128)(2,1)} %bitcast.13, s32[4,64]{1,0:T(4,128)} %bitcast.14, s32[1,32]{1,0:T(1,128)} %bitcast.15), custom_call_target="tpu_custom_call" | custom-call | tf_op jit(solution)/shard_map/pallas_call | solution.py:272
  37.4 1.8 %copy.11 = f32[3,16,16,128]{3,2,1,0:T(8,128)} copy(f32[3,16,16,128]{3,2,1,0:T(8,128)} %bitcast.11) | data formatting | bytes 786432
  39.1 1.8 %copy.12 = f32[3,16,16,128]{3,2,1,0:T(8,128)} copy(f32[3,16,16,128]{3,2,1,0:T(8,128)} %bitcast.10) | data formatting | bytes 786432

commit v2 on v1

--- a/solution.py
+++ b/solution.py
@@ -34,10 +34,12 @@
     res_hbm, stiff_ref, inv_hbm, basis_ref, crows_ref, lists_ref, pmap_ref,
     sol_ref, fin_ref,
     res_v, inv_v, sub, sel, selt, outs, backs, backr, hs, hr, allbuf,
-    sext, bsend, brecv, bext, diag, m_lo, m_hi, xs, mid,
+    sext, bsend, brecv, bextf, cmat, csend, diag, m_lo, m_hi, xs, mid,
     lsem, nsem_s, nsem_r, csem_s, csem_r, g1s, g1r, g2s, g2r,
 ):
     comps, cx, cy, nv = dims
+    halo = hr.shape[2]
+    hrows = (comps * cy, comps * cy, comps * cx, comps * cx)
     own = comps * cx * cy
     layer = cx * cy
     ov = lists_ref.shape[1]
@@ -95,7 +97,7 @@
         def _(p=p, at=at):
             for t in range(2):
                 sub[t, at : at + ov, :] = jnp.zeros((ov, nv), BF16)
-                hr[t, p] = jnp.zeros(hr.shape[2:], F32)
+                hr[t, p] = jnp.zeros(hr.shape[2:], BF16)
 
         @pl.when(jnp.logical_not(has_up[p]))
         def _(p=p):
@@ -103,6 +105,12 @@
                 backr[t, p * ov : (p + 1) * ov, :] = jnp.zeros((ov, nv), BF16)
             sext[(p + 1) * kw : (p + 2) * kw, :] = jnp.zeros((kw, kd), F32)
             brecv[p * kw : (p + 1) * kw, :] = jnp.zeros((kw, 4 * ov), F32)
+
+        @pl.when(jnp.logical_not(has_down[p]))
+        def _(p=p):
+            cmat[own + p * halo : own + (p + 1) * halo, :] = jnp.zeros((halo, kd), BF16)
+
+    sext[5 * kw :, :] = jnp.zeros((sext.shape[0] - 5 * kw, kd), F32)
 
     load_res.wait()
 
@@ -159,6 +167,14 @@
     m_lo[...] = jnp.where(second == 0.0, 0.0, 1.0)
     m_hi[...] = jnp.where(second == cy - 1.0, 0.0, 1.0)
 
+    def layer_rows(ref, p):
+        if p >= 2:
+            return ref[pl.ds((cy - 1) * (3 - p), comps * cx, stride=cy), :]
+        skip = (layer - cy) * (1 - p)
+        return jnp.concatenate([ref[c * layer + skip : c * layer + skip + cy, :] for c in range(comps)], axis=0)
+
+    wait_edges = []
+
     def correct(t, src, dst, wait_margins):
         if t == 0:
             load_inv.wait()
@@ -187,25 +203,51 @@
             False,
         )
         xs[...] = patch[:own]
-        for o in range(1, gx):
-            stage1(o, lax.rem(a + o, gx), lax.rem(a + (gx - o), gx)).wait_recv()
-        for o in range(1, gy):
-            stage2(o, lax.rem(b + o, gy), b).start()
         if t == 0:
             wait_coarse()
             rb = fdiv(fiota((4 * kw, 4 * ov), 0), kw)
             cb = fdiv(fiota((4 * kw, 4 * ov), 1), ov)
             margins = jnp.where(rb == cb, brecv[...], 0.0).astype(BF16)
             below = dot(margins, selt[...])
-            ext = jnp.concatenate([basis_ref[:, :own].astype(F32), below], axis=0)
-            bext[...] = ext.T.astype(BF16)
+            rest = jnp.zeros((sext.shape[0] - 5 * kw, own), F32)
+            ext = jnp.concatenate([basis_ref[:, :own].astype(F32), below, rest], axis=0)
+            bextf[...] = ext.T
+            edges = jnp.concatenate([layer_rows(bextf, p) for p in range(4)], axis=0).astype(BF16)
+
+            def build(c, _):
+                at = pl.ds(pl.multiple_of(c * wide, wide), wide)
+                part_s = sext[:, at].astype(BF16)
+                csend[:, at] = dot(edges, part_s).astype(BF16)
+                cmat[:own, at] = dot(bextf[...].astype(BF16), part_s).astype(BF16)
+                return 0
+
+            lax.fori_loop(jnp.int32(0), jnp.int32(kd // wide), build, 0)
+            wait_edges.append(trade(
+                lambda p: [remote(csend.at[pl.ds(p * halo, halo)], cmat.at[pl.ds(own + p * halo, halo)],
+                                  csem_s.at[2, p], csem_r.at[2, p], up[p])],
+                True,
+            ))
+        for o in range(1, gx):
+            stage1(o, lax.rem(a + o, gx), lax.rem(a + (gx - o), gx)).wait_recv()
+        for o in range(1, gy):
+            stage2(o, lax.rem(b + o, gy), b).start()
         wait_back()
         xs[...] += dot(sel[...], backr[t])
+
+        for p in range(4):
+            hs[t, p, : hrows[p], :] = layer_rows(xs, p).astype(hs.dtype)
+        wait_halo = trade(
+            lambda p: [remote(hs.at[t, p], hr.at[t, p], nsem_s.at[t, 2, p], nsem_r.at[t, 2, p], up[p])],
+            True,
+        )
+        if t == 0:
+            wait_edges[0]()
         for o in range(1, gy):
             stage2(o, lax.rem(b + o, gy), lax.rem(b + (gy - o), gy)).wait_recv()
         gathered = allbuf[t].astype(F32).reshape(kd, nv).astype(BF16)
-        cout = dot(sext[...].astype(BF16), gathered).astype(BF16)
-        xs[...] += dot(bext[...], cout)
+        coarse = dot(cmat[...], gathered)
+        xs[...] += coarse[:own]
+        far = coarse[own:]
 
         def done():
             for o in range(1, gx):
@@ -215,16 +257,6 @@
 
         finish.append(done)
 
-        for c in range(comps):
-            base = c * layer
-            hs[t, 0, c * cy : (c + 1) * cy, :] = xs[base + layer - cy : base + layer, :]
-            hs[t, 1, c * cy : (c + 1) * cy, :] = xs[base : base + cy, :]
-        hs[t, 2, : comps * cx, :] = xs[pl.ds(cy - 1, comps * cx, stride=cy), :]
-        hs[t, 3, : comps * cx, :] = xs[pl.ds(0, comps * cx, stride=cy), :]
-        wait_halo = trade(
-            lambda p: [remote(hs.at[t, p], hr.at[t, p], nsem_s.at[t, 2, p], nsem_r.at[t, 2, p], up[p])],
-            True,
-        )
         zero = jnp.zeros((cy, nv), F32)
         for c in range(comps):
             at = pl.ds(c * layer, layer)
@@ -232,26 +264,23 @@
             beside = jnp.concatenate([zero, x[:-cy]], axis=0) + jnp.concatenate([x[cy:], zero], axis=0)
             beside += pltpu.roll(x, 1, 0) * m_lo[...] + pltpu.roll(x, layer - 1, 0) * m_hi[...]
             dst[at, :] = src[at, :] - (diag[...] * x - beside)
-        return wait_halo
-
-    def finish_halo(t, dst, wait_halo):
         wait_halo()
+        around = [hr[t, p, : hrows[p], :].astype(F32) + far[p * halo : p * halo + hrows[p]] for p in range(4)]
         for c in range(comps):
             base = c * layer
-            dst[base : base + cy, :] += hr[t, 0, c * cy : (c + 1) * cy, :]
-            dst[base + layer - cy : base + layer, :] += hr[t, 1, c * cy : (c + 1) * cy, :]
+            dst[base : base + cy, :] += around[0][c * cy : (c + 1) * cy]
+            dst[base + layer - cy : base + layer, :] += around[1][c * cy : (c + 1) * cy]
         low = pl.ds(0, comps * cx, stride=cy)
         high = pl.ds(cy - 1, comps * cx, stride=cy)
-        dst[low, :] = dst[low, :] + hr[t, 2, : comps * cx, :]
-        dst[high, :] = dst[high, :] + hr[t, 3, : comps * cx, :]
-
-    wait_halo = correct(0, res_v, mid, wait_margins)
+        dst[low, :] = dst[low, :] + around[2]
+        dst[high, :] = dst[high, :] + around[3]
+
+    correct(0, res_v, mid, wait_margins)
+    gather(1, mid)
+    wait_margins = start_margins(1)
     sol_ref[...] = xs[...]
-    finish_halo(0, mid, wait_halo)
-    gather(1, mid)
-    wait_halo = correct(1, mid, fin_ref, start_margins(1))
+    correct(1, mid, fin_ref, wait_margins)
     sol_ref[...] += xs[...]
-    finish_halo(1, fin_ref, wait_halo)
     for end in finish:
         end()
 
@@ -266,6 +295,7 @@
         ov = send_rows.shape[-1]
         kw, kd = coarse_rows.shape[-2:]
         halo = comps * max(cx, cy)
+        lanes = -(-5 * kw // 128) * 128
         vm = pl.BlockSpec(memory_space=pltpu.VMEM)
         anywhere = pl.BlockSpec(memory_space=pl.ANY)
         dma = pltpu.SemaphoreType.DMA
@@ -283,13 +313,15 @@
                 pltpu.VMEM((2, 4 * ov, nv), BF16),
                 pltpu.VMEM((2, 4 * ov, nv), BF16),
                 pltpu.VMEM((2, 4 * ov, nv), BF16),
-                pltpu.VMEM((2, 4, halo, nv), F32),
-                pltpu.VMEM((2, 4, halo, nv), F32),
+                pltpu.VMEM((2, 4, halo, nv), BF16),
+                pltpu.VMEM((2, 4, halo, nv), BF16),
                 pltpu.VMEM((2, gy, gx, kw, nv), BF16),
-                pltpu.VMEM((5 * kw, kd), F32),
+                pltpu.VMEM((lanes, kd), F32),
                 pltpu.VMEM((kw, m - own), F32),
                 pltpu.VMEM((4 * kw, m - own), F32),
-                pltpu.VMEM((own, 5 * kw), BF16),
+                pltpu.VMEM((own, lanes), F32),
+                pltpu.VMEM((own + 4 * halo, kd), BF16),
+                pltpu.VMEM((4 * halo, kd), BF16),
                 pltpu.VMEM((layer, nv), F32),
                 pltpu.VMEM((layer, nv), F32),
                 pltpu.VMEM((layer, nv), F32),
@@ -298,8 +330,8 @@
                 dma((2,)),
                 dma((2, 3, 4)),
                 dma((2, 3, 4)),
-                dma((2, 4)),
-                dma((2, 4)),
+                dma((3, 4)),
+                dma((3, 4)),
                 dma((2, gx)),
                 dma((2, gx)),
                 dma((2, gy)),

time: 41.2 us -> 35.7 us (0.87)
  Pallas kernels: 36.7 us -> 31.3 us
    pallas_call x1, Pallas kernels: 36.7 us -> 31.3 us  [per_device(): pl.pallas_call(functools.partial(kernel, gx, gy, (comps, cx, cy, nv)), ou...]
where the time goes in v2:
time: 35.7 us; the launch traced here: 35.4 us
  Pallas kernels  31.3 us (88%)
  local copies, waits for them, and re-layouts  3.53 us (10%)
  between operations  0.64 us (2%)
    pallas_call x1, Pallas kernels, per_device(): pl.pallas_call(functools.partial(kernel, gx, gy, (comps, cx, cy, nv)), ou...  31.3 us
    unnamed x2, local copies, waits for them, and re-layouts  3.53 us

profile of v2, /device:TPU:0, one launch (start us, length us, event | category | flops | bytes accessed | tf_op | source)
XLA Modules:
  0.0 35.4 jit_solution(6020549846329125328)
XLA Ops:
  0.6 31.3 %shard_map.86 = (f32[768,128]{1,0:T(8,128)}, f32[768,128]{1,0:T(8,128)}) custom-call(f32[768,128]{1,0:T(8,128)} %bitcast.9, f32[16,16]{1,0:T(8,128)} %stiff_ref.1, bf16[1024,1024]{1,0:T(8,128)(2,1)} %bitcast.8, bf16[8,1024]{1,0:T(8,128)(2,1)} %bitcast.12, bf16[8,256]{1,0:T(8,128)(2,1)} %bitcast.13, s32[4,64]{1,0:T(4,128)} %bitcast.14, s32[1,32]{1,0:T(1,128)} %bitcast.15), custom_call_target="tpu_custom_call" | custom-call | tf_op jit(solution)/shard_map/pallas_call | solution.py:302
  31.9 1.8 %copy.11 = f32[3,16,16,128]{3,2,1,0:T(8,128)} copy(f32[3,16,16,128]{3,2,1,0:T(8,128)} %bitcast.11) | data formatting | bytes 786432
  33.7 1.8 %copy.12 = f32[3,16,16,128]{3,2,1,0:T(8,128)} copy(f32[3,16,16,128]{3,2,1,0:T(8,128)} %bitcast.10) | data formatting | bytes 786432

commit v3 on v2

--- a/solution.py
+++ b/solution.py
@@ -31,10 +31,10 @@
 
 def kernel(
     gx, gy, dims,
-    res_hbm, stiff_ref, inv_hbm, basis_ref, crows_ref, lists_ref, pmap_ref,
+    res_hbm, stiff_hbm, inv_hbm, basis_hbm, crows_hbm, lists_hbm, pmap_hbm,
     sol_ref, fin_ref,
-    res_v, inv_v, sub, sel, selt, outs, backs, backr, hs, hr, allbuf,
-    sext, bsend, brecv, bextf, cmat, csend, diag, m_lo, m_hi, xs, mid,
+    res_v, stiff_ref, inv_v, basis_ref, crows_ref, lists_ref, pmap_ref, sub, sel, selt, outs, backs, backr, hs, hr, allbuf,
+    sext, bsend, brecv, bextf, cmat, acmat, csend, diag, m_lo, m_hi, xs, mid,
     lsem, nsem_s, nsem_r, csem_s, csem_r, g1s, g1r, g2s, g2r,
 ):
     comps, cx, cy, nv = dims
@@ -47,17 +47,21 @@
     a = lax.axis_index("gx")
     b = lax.axis_index("gy")
 
-    load_res = pltpu.make_async_copy(res_hbm, res_v, lsem.at[0])
-    load_inv = pltpu.make_async_copy(inv_hbm, inv_v, lsem.at[1])
-    load_res.start()
-    load_inv.start()
-
+    wanted = [
+        (lists_hbm, lists_ref), (res_hbm, res_v), (pmap_hbm, pmap_ref), (crows_hbm, crows_ref),
+        (basis_hbm, basis_ref), (stiff_hbm, stiff_ref), (inv_hbm, inv_v),
+    ]
+    loads = [pltpu.make_async_copy(x, y, lsem.at[k]) for k, (x, y) in enumerate(wanted)]
+    load_lists, load_res, load_pmap, load_crows, load_basis, load_stiff, load_inv = loads
     barrier = pltpu.get_barrier_semaphore()
     for o in range(1, gx):
         pl.semaphore_signal(barrier, inc=1, device_id=(lax.rem(a + o, gx), b), device_id_type=MESH)
     for o in range(1, gy):
         pl.semaphore_signal(barrier, inc=1, device_id=(a, lax.rem(b + o, gy)), device_id_type=MESH)
 
+    for load in loads:
+        load.start()
+
     up = [(a + 1, b), (a - 1, b), (a, b + 1), (a, b - 1)]
     has_up = [a < gx - 1, a > 0, b < gy - 1, b > 0]
     down = [up[p ^ 1] for p in range(4)]
@@ -65,7 +69,7 @@
     finish = []
 
     def send(copies, conds, wait):
-        for p in range(4):
+        for p in (2, 3, 0, 1):
             @pl.when(conds[p])
             def _(p=p):
                 for c in copies(p):
@@ -82,6 +86,7 @@
             src_ref=src, dst_ref=dst, send_sem=s, recv_sem=r, device_id=dev, device_id_type=MESH
         )
 
+    load_lists.wait()
     rows = fiota((own, ov), 0)
     lists = lists_ref[...].astype(F32)
     for h in range(2):
@@ -131,6 +136,9 @@
 
     wait_margins = start_margins(0)
 
+    load_pmap.wait()
+    load_crows.wait()
+    load_basis.wait()
     wide = min(kd, 256)
     n = gx * gy
     pmf = jnp.broadcast_to(pmap_ref[...].astype(F32), (8, n))
@@ -156,6 +164,7 @@
         False,
     )
 
+    load_stiff.wait()
     r1 = fiota((layer, cy), 0)
     first = fdiv(r1, cy)
     mine = jnp.where(fiota((layer, cx), 1) == fdiv(fiota((layer, cx), 0), cy), 1.0, 0.0)
@@ -172,6 +181,26 @@
             return ref[pl.ds((cy - 1) * (3 - p), comps * cx, stride=cy), :]
         skip = (layer - cy) * (1 - p)
         return jnp.concatenate([ref[c * layer + skip : c * layer + skip + cy, :] for c in range(comps)], axis=0)
+
+    def operate(x_ref, dst, src):
+        zero = jnp.zeros((cy, nv), F32)
+        for c in range(comps):
+            at = pl.ds(c * layer, layer)
+            x = x_ref[at, :]
+            beside = jnp.concatenate([zero, x[:-cy]], axis=0) + jnp.concatenate([x[cy:], zero], axis=0)
+            beside += pltpu.roll(x, 1, 0) * m_lo[...] + pltpu.roll(x, layer - 1, 0) * m_hi[...]
+            value = beside - diag[...] * x
+            dst[at, :] = value if src is None else src[at, :] + value
+
+    def add_layers(dst, around):
+        for c in range(comps):
+            base = c * layer
+            dst[base : base + cy, :] += around(0)[c * cy : (c + 1) * cy]
+            dst[base + layer - cy : base + layer, :] += around(1)[c * cy : (c + 1) * cy]
+        low = pl.ds(0, comps * cx, stride=cy)
+        high = pl.ds(cy - 1, comps * cx, stride=cy)
+        dst[low, :] = dst[low, :] + around(2)
+        dst[high, :] = dst[high, :] + around(3)
 
     wait_edges = []
 
@@ -218,7 +247,6 @@
                 at = pl.ds(pl.multiple_of(c * wide, wide), wide)
                 part_s = sext[:, at].astype(BF16)
                 csend[:, at] = dot(edges, part_s).astype(BF16)
-                cmat[:own, at] = dot(bextf[...].astype(BF16), part_s).astype(BF16)
                 return 0
 
             lax.fori_loop(jnp.int32(0), jnp.int32(kd // wide), build, 0)
@@ -240,14 +268,28 @@
             lambda p: [remote(hs.at[t, p], hr.at[t, p], nsem_s.at[t, 2, p], nsem_r.at[t, 2, p], up[p])],
             True,
         )
+        operate(xs, dst, src)
         if t == 0:
             wait_edges[0]()
+            bext = bextf[...].astype(BF16)
+
+            def fill(c, _):
+                at = pl.ds(pl.multiple_of(c * nv, nv), nv)
+                value = dot(bext, sext[:, at].astype(BF16))
+                cmat[:own, at] = value.astype(BF16)
+                sol_ref[...] = value
+                operate(sol_ref, fin_ref, None)
+                add_layers(fin_ref, lambda p: cmat[own + p * halo : own + p * halo + hrows[p], at].astype(F32))
+                acmat[:, at] = fin_ref[...].astype(BF16)
+                return 0
+
+            lax.fori_loop(jnp.int32(0), jnp.int32(kd // nv), fill, 0)
+        wait_halo()
+        add_layers(dst, lambda p: hr[t, p, : hrows[p], :].astype(F32))
         for o in range(1, gy):
             stage2(o, lax.rem(b + o, gy), lax.rem(b + (gy - o), gy)).wait_recv()
         gathered = allbuf[t].astype(F32).reshape(kd, nv).astype(BF16)
-        coarse = dot(cmat[...], gathered)
-        xs[...] += coarse[:own]
-        far = coarse[own:]
+        dst[...] += dot(acmat[...], gathered)
 
         def done():
             for o in range(1, gx):
@@ -257,30 +299,14 @@
 
         finish.append(done)
 
-        zero = jnp.zeros((cy, nv), F32)
-        for c in range(comps):
-            at = pl.ds(c * layer, layer)
-            x = xs[at, :]
-            beside = jnp.concatenate([zero, x[:-cy]], axis=0) + jnp.concatenate([x[cy:], zero], axis=0)
-            beside += pltpu.roll(x, 1, 0) * m_lo[...] + pltpu.roll(x, layer - 1, 0) * m_hi[...]
-            dst[at, :] = src[at, :] - (diag[...] * x - beside)
-        wait_halo()
-        around = [hr[t, p, : hrows[p], :].astype(F32) + far[p * halo : p * halo + hrows[p]] for p in range(4)]
-        for c in range(comps):
-            base = c * layer
-            dst[base : base + cy, :] += around[0][c * cy : (c + 1) * cy]
-            dst[base + layer - cy : base + layer, :] += around[1][c * cy : (c + 1) * cy]
-        low = pl.ds(0, comps * cx, stride=cy)
-        high = pl.ds(cy - 1, comps * cx, stride=cy)
-        dst[low, :] = dst[low, :] + around[2]
-        dst[high, :] = dst[high, :] + around[3]
-
-    correct(0, res_v, mid, wait_margins)
+        return gathered
+
+    gathered = correct(0, res_v, mid, wait_margins)
     gather(1, mid)
     wait_margins = start_margins(1)
-    sol_ref[...] = xs[...]
-    correct(1, mid, fin_ref, wait_margins)
-    sol_ref[...] += xs[...]
+    sol_ref[...] = xs[...] + dot(cmat[:own, :], gathered)
+    gathered = correct(1, mid, fin_ref, wait_margins)
+    sol_ref[...] += xs[...] + dot(cmat[:own, :], gathered)
     for end in finish:
         end()
 
@@ -301,12 +327,17 @@
         dma = pltpu.SemaphoreType.DMA
         out = pl.pallas_call(
             functools.partial(kernel, gx, gy, (comps, cx, cy, nv)),
-            out_shape=[jax.ShapeDtypeStruct((own, nv), F32)] * 2,
-            in_specs=[anywhere, vm, anywhere, vm, vm, vm, vm],
+            out_shape=[pltpu.VMEM((own, nv), F32)] * 2,
+            in_specs=[anywhere] * 7,
             out_specs=[vm, vm],
             scratch_shapes=[
                 pltpu.VMEM((own, nv), F32),
+                pltpu.VMEM((cx, cy), F32),
                 pltpu.VMEM((m, m), BF16),
+                pltpu.VMEM((kw, m), BF16),
+                pltpu.VMEM((kw, kd), BF16),
+                pltpu.VMEM((4, ov), jnp.int32),
+                pltpu.VMEM((1, gx * gy), jnp.int32),
                 pltpu.VMEM((2, m, nv), BF16),
                 pltpu.VMEM((own, 4 * ov), BF16),
                 pltpu.VMEM((4 * ov, own), BF16),
@@ -321,13 +352,14 @@
                 pltpu.VMEM((4 * kw, m - own), F32),
                 pltpu.VMEM((own, lanes), F32),
                 pltpu.VMEM((own + 4 * halo, kd), BF16),
+                pltpu.VMEM((own, kd), BF16),
                 pltpu.VMEM((4 * halo, kd), BF16),
                 pltpu.VMEM((layer, nv), F32),
                 pltpu.VMEM((layer, nv), F32),
                 pltpu.VMEM((layer, nv), F32),
                 pltpu.VMEM((own, nv), F32),
                 pltpu.VMEM((own, nv), F32),
-                dma((2,)),
+                dma((7,)),
                 dma((2, 3, 4)),
                 dma((2, 3, 4)),
                 dma((3, 4)),

time: 35.7 us -> 32.1 us (0.90)
  local copies, waits for them, and re-layouts: 3.53 us -> 1.49 us
  Pallas kernels: 31.3 us -> 29.8 us
    unnamed x2, local copies, waits for them, and re-layouts: 3.53 us -> 1.49 us
    pallas_call x1, Pallas kernels: 31.3 us -> 29.8 us  [per_device(): pl.pallas_call(functools.partial(kernel, gx, gy, (comps, cx, cy, nv)), ou...]
where the time goes in v3:
time: 32.1 us; the launch traced here: 31.9 us
  Pallas kernels  29.8 us (93%)
  local copies, waits for them, and re-layouts  1.49 us (5%)
  between operations  0.64 us (2%)
    pallas_call x1, Pallas kernels, per_device(): pl.pallas_call(functools.partial(kernel, gx, gy, (comps, cx, cy, nv)), ou...  29.8 us
    unnamed x2, local copies, waits for them, and re-layouts  1.49 us

profile of v3, /device:TPU:0, one launch (start us, length us, event | category | flops | bytes accessed | tf_op | source)
XLA Modules:
  0.0 31.9 jit_solution(15607267057312603405)
XLA Ops:
  0.6 29.8 %shard_map.86 = (f32[768,128]{1,0:T(8,128)S(1)}, f32[768,128]{1,0:T(8,128)S(1)}) custom-call(f32[768,128]{1,0:T(8,128)} %bitcast.11, f32[16,16]{1,0:T(8,128)} %stiff_hbm.1, bf16[1024,1024]{1,0:T(8,128)(2,1)} %bitcast.10, bf16[8,1024]{1,0:T(8,128)(2,1)} %bitcast.12, bf16[8,256]{1,0:T(8,128)(2,1)} %bitcast.13, s32[4,64]{1,0:T(4,128)} %bitcast.14, s32[1,32]{1,0:T(1,128)} %bitcast.15), custom_call_target="tpu_custom_call" | custom-call | tf_op jit(solution)/shard_map/pallas_call | solution.py:328
  30.4 0.7 %copy.11 = f32[3,16,16,128]{3,2,1,0:T(8,128)} copy(f32[3,16,16,128]{3,2,1,0:T(8,128)S(1)} %bitcast.9) | data formatting | bytes 786432
  31.2 0.7 %copy.12 = f32[3,16,16,128]{3,2,1,0:T(8,128)} copy(f32[3,16,16,128]{3,2,1,0:T(8,128)S(1)} %bitcast.8) | data formatting | bytes 786432

commit v4 on v3

--- a/solution.py
+++ b/solution.py
@@ -224,14 +224,13 @@
 
         for o in range(1, gx):
             stage1(o, lax.rem(a + o, gx), a).start()
-        patch = part + dot(inv_v[:, own:], edge)
-        backs[t] = patch[own:].astype(BF16)
+        backs[t] = (part[own:] + dot(inv_v[own:, own:], edge)).astype(BF16)
         wait_back = trade(
             lambda p: [remote(backs.at[t, pl.ds(p * ov, ov)], backr.at[t, pl.ds(p * ov, ov)],
                               nsem_s.at[t, 1, p], nsem_r.at[t, 1, p], down[p])],
             False,
         )
-        xs[...] = patch[:own]
+        xs[...] = part[:own] + dot(inv_v[:own, own:], edge)
         if t == 0:
             wait_coarse()
             rb = fdiv(fiota((4 * kw, 4 * ov), 0), kw)

time: 32.1 us -> 31.4 us (0.978)
  Pallas kernels: 29.8 us -> 29 us
    pallas_call x1, Pallas kernels: 29.8 us -> 29 us  [per_device(): pl.pallas_call(functools.partial(kernel, gx, gy, (comps, cx, cy, nv)), ou...]
where the time goes in v4:
time: 31.4 us; the launch traced here: 31.2 us
  Pallas kernels  29 us (92%)
  local copies, waits for them, and re-layouts  1.49 us (5%)
  between operations  0.64 us (2%)
    pallas_call x1, Pallas kernels, per_device(): pl.pallas_call(functools.partial(kernel, gx, gy, (comps, cx, cy, nv)), ou...  29 us
    unnamed x2, local copies, waits for them, and re-layouts  1.49 us

profile of v4, /device:TPU:0, one launch (start us, length us, event | category | flops | bytes accessed | tf_op | source)
XLA Modules:
  0.0 31.2 jit_solution(15029759236386915702)
XLA Ops:
  0.6 29.0 %shard_map.86 = (f32[768,128]{1,0:T(8,128)S(1)}, f32[768,128]{1,0:T(8,128)S(1)}) custom-call(f32[768,128]{1,0:T(8,128)} %bitcast.11, f32[16,16]{1,0:T(8,128)} %stiff_hbm.1, bf16[1024,1024]{1,0:T(8,128)(2,1)} %bitcast.10, bf16[8,1024]{1,0:T(8,128)(2,1)} %bitcast.12, bf16[8,256]{1,0:T(8,128)(2,1)} %bitcast.13, s32[4,64]{1,0:T(4,128)} %bitcast.14, s32[1,32]{1,0:T(1,128)} %bitcast.15), custom_call_target="tpu_custom_call" | custom-call | tf_op jit(solution)/shard_map/pallas_call | solution.py:327
  29.7 0.7 %copy.11 = f32[3,16,16,128]{3,2,1,0:T(8,128)} copy(f32[3,16,16,128]{3,2,1,0:T(8,128)S(1)} %bitcast.9) | data formatting | bytes 786432
  30.4 0.7 %copy.12 = f32[3,16,16,128]{3,2,1,0:T(8,128)} copy(f32[3,16,16,128]{3,2,1,0:T(8,128)S(1)} %bitcast.8) | data formatting | bytes 786432
